TPU v7x, 256 devices: a whole 4x4x8 slice. The times are simulated.
256 devices in a mesh: rows: 16 (over z_lo, y, core), tm: 16 (over x, z_hi).
Axes of the slice: x: 4, y: 4, z: 8 (z_hi: 4, z_lo: 2; z = z_hi * 2 + z_lo), core: 2. Of those that a mesh axis runs over, the one named last changes fastest.
Arguments:
- residual: float32 [64, 1024, 512], P('tm', 'rows'), may hold values from -45 to 45
- cycle_weight: float32 [64, 1024, 512], P('tm', 'rows'), may hold values from -0.75 to 0.75
- cycle_offsets: int32 [64, 2], replicated, may hold values from -6 to 6, as said below
Outputs:
- new_weight: float32 [64, 1024, 512], P('tm', 'rows')
- error: float32 [64, 1024, 512], P('tm', 'rows')
Inputs may be any that keep to these rules, and one draw needn't show every extreme that they name: `cycle_offsets`: each row is a distinct (row, column) offset; together the rows are the 64 pixels (dy, dx) with 17 <= dy*dy + dx*dx <= 36, in an order drawn from the seed.
All inputs are finite; a program needn't handle non-finite values.
Results may differ from a plain program's by a relative error of at most 0.0003.
Values sent between devices are 32-bit elements; how exact they have to be, the bound alone decides.
A program may use at most 64 MiB of HBM per device.

v0:
```python
import jax
import jax.numpy as jnp
import numpy as np
from jax import lax
from jax.sharding import PartitionSpec as P


def with_halo(cells, sides, width):
    for axis, dim in sides:
        count = lax.axis_size(axis)
        ends = count - 1
        head = lax.slice_in_dim(cells, 0, width, axis=dim)
        tail = lax.slice_in_dim(cells, cells.shape[dim] - width, cells.shape[dim], axis=dim)
        cells = jnp.concatenate(
            [
                lax.ppermute(tail, axis, [(i, (i + 1) % count) for i in range(ends)]),
                cells,
                lax.ppermute(head, axis, [((i + 1) % count, i) for i in range(ends)]),
            ],
            axis=dim,
        )
    return cells


def cycle_points():
    points = []
    for row_off in range(-6, 7):
        for col_off in range(-6, 7):
            radius = row_off * row_off + col_off * col_off
            if radius >= 17 and radius <= 36:
                points.append((row_off, col_off))
    return points


def matching(cycle_offsets, points):
    table_rows = jnp.asarray(np.array([p[0] for p in points], dtype=np.int32))
    table_cols = jnp.asarray(np.array([p[1] for p in points], dtype=np.int32))
    same = (table_rows[:, None] == cycle_offsets[None, :, 0]) & (
        table_cols[:, None] == cycle_offsets[None, :, 1]
    )
    return same.astype(jnp.float32)


def reorder(selector, weights):
    return jnp.einsum("jk,kyx->jyx", selector, weights, precision=lax.Precision.HIGHEST)


def window_of(padded, point, height, width):
    return padded[:, 6 + point[0] : 6 + point[0] + height, 6 + point[1] : 6 + point[1] + width]


def cycle_passes(padded, centre, ordered_weight, points, height, width):
    background = jnp.zeros(centre.shape, jnp.float32)
    for index, point in enumerate(points):
        background = background + ordered_weight[index][None] * window_of(
            padded, point, height, width
        )
    error_part = centre - background
    grads = jnp.stack(
        [jnp.sum(error_part * window_of(padded, point, height, width), axis=0) for point in points]
    )
    squares = jnp.sum(padded * padded, axis=0)
    energy_sum = jnp.zeros((height, width), jnp.float32)
    for point in points:
        energy_sum = (
            energy_sum
            + squares[6 + point[0] : 6 + point[0] + height, 6 + point[1] : 6 + point[1] + width]
        )
    return (error_part, grads, energy_sum)


def on_device(residual, cycle_weight, cycle_offsets):
    frames_dev, rows_dev, cols = residual.shape
    cycle = cycle_offsets.shape[0]
    tm_count = lax.axis_size("tm")
    frames_all = frames_dev * tm_count
    points = cycle_points()
    selector = matching(cycle_offsets, points)
    extended = with_halo(residual, (("rows", 1),), 6)
    padded = jnp.pad(extended, ((0, 0), (0, 0), (6, 6)))
    columns = selector
    ordered_weight = reorder(columns, lax.all_gather(cycle_weight, "tm", axis=0, tiled=True))
    error, ordered_grad, local_energy = cycle_passes(
        padded, residual, ordered_weight, points, rows_dev, cols
    )
    columns = selector
    gradient = lax.psum_scatter(
        jnp.einsum("jk,jyx->kyx", columns, ordered_grad, precision=lax.Precision.HIGHEST),
        "tm",
        scatter_dimension=0,
        tiled=True,
    )
    energy = lax.psum(local_energy, "tm") / (cycle * frames_all) + 1e-06
    new_weight = cycle_weight + gradient / (frames_all * energy)[None]
    return (new_weight, error)


def solution(mesh):
    in_specs = (P("tm", "rows", None), P("tm", "rows", None), P())
    out_specs = (P("tm", "rows", None), P("tm", "rows", None))
    return jax.shard_map(
        on_device, mesh=mesh, in_specs=in_specs, out_specs=out_specs, check_vma=False
    )
```

profile of v0, /device:TPU:4, one launch (start us, length us, event | category | flops | bytes accessed | tf_op | source)
XLA Modules:
  0.0 429.7 jit_solution(9261241765014633690)
XLA Ops:
  8.0 0.9 fusion.19
  8.9 1.7 collective-permute-start
  10.6 1.3 collective-permute-start.1
  11.9 0.8 slice_bitcast_fusion.1
  12.7 1.1 constant_dynamic-update-slice_fusion.1
  13.8 1.4 collective-permute-done.1
  15.1 1.4 multiply_reduce_fusion
  16.5 2.8 slice_add_fusion
  19.9 97.1 %all-gather.2.cloned.1.call-done = f32[64,64,512]{2,1,0:T(8,128)} async-done(((f32[4,64,512]{2,1,0:T(8,128)}), f32[64,64,512]{2,1,0:T(8,128)}) %all-gather.2.cloned.1.call-update) | async-done | bytes 8388624 | tf_op jit(solution)/shard_map/all_gather | solution.py:82
  117.0 13.4 %fusion = f32[64,64,512]{2,0,1:T(8,128)S(1)} fusion(f32[64,64,512]{2,1,0:T(8,128)} %all-gather.2.cloned.1.call-done, s32[64]{0:T(128)S(1)} %copy-done.4, s32[64]{0:T(128)S(1)} %copy-done.3, s32[64]{0:T(128)S(1)} %get-tuple-element.146, s32[64]{0:T(128)S(1)} %get-tuple-element.145), kind=kOutput, calls=%fused_computation | convolution fusion | flops 1610625024 | bytes 16778240 | tf_op jit(solution)/shard_map/jk,kyx->jyx/dot_general | solution.py:45
  130.5 2.0 fusion.17
  132.4 2.3 fusion.15
  134.7 2.4 fusion.16
  138.8 9.4 %multiply_reduce_fusion.2 = (f32[64,512]{1,0:T(8,128)S(1)}, f32[64,512]{1,0:T(8,128)S(1)}, f32[64,512]{1,0:T(8,128)S(1)}, f32[64,512]{1,0:T(8,128)S(1)}, f32[64,...) fusion(f32[4,76,524]{2,1,0:T(8,128)S(1)} %get-tuple-element.142, ...), kind=kLoop, calls=%fused_computation.14 | loop fusion | flops 21168128 | bytes 44351488 | tf_op jit(solution)/shard_map/reduce_sum | solution.py:60
  148.3 2.5 multiply_reduce_fusion.39
  150.8 2.4 multiply_reduce_fusion.21
  154.3 0.7 stack.214
  155.0 0.7 stack.215
  156.5 0.7 stack.217
  157.9 0.7 stack.219
  158.7 0.7 stack.220
  159.4 0.7 stack.221
  161.6 0.7 stack.224
  163.1 0.7 stack.226
  163.9 0.7 stack.227
  164.6 0.7 stack.228
  166.1 0.7 stack.230
  166.8 0.7 stack.231
  167.6 0.7 stack.232
  168.3 0.7 stack.233
  169.1 0.7 stack.234
  171.3 0.7 stack.237
  172.0 0.7 stack.238
  172.7 0.9 multiply_reduce_fusion.1
  178.7 0.8 stack.248
  179.4 0.7 stack.249
  181.7 0.7 stack.252
  182.4 0.7 stack.253
  183.1 1.0 stack.255
  184.1 0.7 stack.256
  184.8 0.7 stack.257
  185.6 28.8 %stack.259 = f32[64,64,512]{2,0,1:T(8,128)} concatenate(f32[1,64,512]{2,0,1:T(1,128)S(1)} %stack.195, f32[1,64,512]{2,0,1:T(1,128)S(1)} %stack.196, f32[1,64,512]{2,0,1:T(1,128)S(1)} %stack.197, f32[1,64,512]{2,0,1:T(1,128)S(1)} %stack.198, f32[1,64,512]{2,0,1:T(1,128)S(1)} %stack.199, f32[1,64,512]{2,0,1:T(1,128)S(1)} %stack.200, f32[1,64,512]{2,0,1:T(1,128)S(1)} %stack.201, ...), dimensions={0} | concatenate | bytes 16777216 | tf_op jit(solution)/shard_map/stack | solution.py:59
  214.3 8.2 %fusion.5 = f32[64,64,512]{2,0,1:T(8,128)S(1)} fusion(f32[64,64,512]{2,0,1:T(8,128)} %stack.259, s32[64]{0:T(128)S(1)} %copy-done.4, s32[64]{0:T(128)S(1)} %copy-done.3, s32[64]{0:T(128)S(1)} %get-tuple-element.146, s32[64]{0:T(128)S(1)} %get-tuple-element.145), kind=kOutput, calls=%fused_computation.207 | convolution fusion | flops 1610625024 | bytes 16778240 | tf_op jit(solution)/shard_map/jk,jyx->kyx/dot_general | solution.py:88
  222.5 8.1 %copy.13 = f32[64,64,512]{2,1,0:T(8,128)} copy(f32[64,64,512]{2,0,1:T(8,128)S(1)} %fusion.5) | data formatting | bytes 16777216 | tf_op jit(solution)/shard_map/jk,jyx->kyx/dot_general | solution.py:88
  230.6 62.9 %all-reduce.3.cloned.1.call-done = f32[64,512]{1,0:T(8,128)} async-done(((f32[64,512]{1,0:T(8,128)}), f32[64,512]{1,0:T(8,128)}) %all-reduce.3.cloned.1.call-update) | async-done | bytes 131088 | tf_op jit(solution)/shard_map/psum | solution.py:93
  293.5 0.9 add_multiply_fusion
  294.4 126.6 %reduce-scatter.2.cloned.1.call-done = f32[4,64,512]{2,1,0:T(8,128)} async-done(((f32[64,64,512]{2,1,0:T(8,128)}), f32[4,64,512]{2,1,0:T(8,128)}) %reduce-scatter.2.cloned.1.call-update) | async-done | bytes 524304 | tf_op jit(solution)/shard_map/reduce_scatter | solution.py:87
  421.0 1.9 divide_add_fusion
  (91 shorter events, 16.0 us)
Async XLA Ops:
  7.2 109.9 %copy-start.3 = (s32[64]{0:T(128)S(1)}, s32[64]{0:T(128)}, u32[]{:S(2)}) copy-start(s32[64]{0:T(128)} %constant.15.clone) | copy-start | bytes 772
  7.2 109.9 %copy-start.4 = (s32[64]{0:T(128)S(1)}, s32[64]{0:T(128)}, u32[]{:S(2)}) copy-start(s32[64]{0:T(128)} %constant.16.clone) | copy-start | bytes 772
  7.2 109.8 %all-gather.2.cloned.1.call-start = ((), (), s32[]{:S(2)}) async-start(), calls=%async_computation.1 | async-start | bytes 8912896 | tf_op jit(solution)/shard_map/all_gather | solution.py:82
  7.9 285.6 %all-reduce.3.cloned.1.call-start = ((), (), s32[]{:S(2)}) async-start(), calls=%async_computation.3 | async-start | bytes 262144 | tf_op jit(solution)/shard_map/psum | solution.py:93
  8.9 4.9 %collective-permute-start = (f32[4,6,512]{2,1,0:T(8,128)S(1)}, f32[4,6,512]{2,1,0:T(8,128)S(1)}, u32[]{:S(2)}, u32[]{:S(2)}) collective-permute-start(f32[4,6,512]{2,1,0:T(8,128)S(1)} %get-tuple-element.143), channel_id=1, source_target_pairs={{0,16},{16,32},{32,48},{48,64},{64,80},{80,96},{96,112},{112,128},... | collective-permute-start | bytes 147464 | tf_op jit(solution)/shard_map/ppermute | solution.py:16
  10.6 4.5 %collective-permute-start.1 = (f32[4,6,512]{2,1,0:T(8,128)S(1)}, f32[4,6,512]{2,1,0:T(8,128)S(1)}, u32[]{:S(2)}, u32[]{:S(2)}) collective-permute-start(f32[4,6,512]{2,1,0:T(8,128)S(1)} %get-tuple-element.144), channel_id=1, source_target_pairs={{16,0},{32,16},{48,32},{64,48},{80,64},{96,80},{112,96},{128,112},... | collective-permute-start | bytes 147464 | tf_op jit(solution)/shard_map/ppermute | solution.py:18
  19.4 401.6 %reduce-scatter.2.cloned.1.call-start = ((), (), s32[]{:S(2)}) async-start(), calls=%async_computation.2 | async-start | bytes 8912896 | tf_op jit(solution)/shard_map/reduce_scatter | solution.py:87
  137.8 1.0 copy-start
  148.3 24.5 %copy-start.1 = (f32[4,64,512]{2,1,0:T(8,128)}, f32[4,64,512]{2,1,0:T(8,128)S(1)}, u32[]{:S(2)}) copy-start(f32[4,64,512]{2,1,0:T(8,128)S(1)} %get-tuple-element.76) | copy-start | bytes 1572868
  230.6 190.4 %copy-start.2 = (f32[4,64,512]{2,1,0:T(8,128)S(1)}, f32[4,64,512]{2,1,0:T(8,128)}, u32[]{:S(2)}) copy-start(f32[4,64,512]{2,1,0:T(8,128)} %param.6) | copy-start | bytes 1572868
Sparse Core Ops, SparseCore 0:
  10.4 106.5 all-gather.1
  119.6 173.7 all-reduce.2
  297.2 123.7 reduce-scatter.1
where the time goes:
time: 434 us; the launch traced here: 430 us
  waiting for transfers between devices  289 us (67%)
  local copies, waits for them, and re-layouts  79 us (18%)
  other arithmetic  22.3 us (5%)
  matrix products  21.6 us (5%)
  between operations  14.6 us (3%)
    reduce_scatter x1, waiting for transfers between devices, on_device(): lax.psum_scatter(jnp.einsum('jk,jyx->kyx', columns, ordered_grad, precisi...  127 us
    all_gather x1, waiting for transfers between devices, on_device(): lax.all_gather(cycle_weight, 'tm', axis=0, tiled=True)  97.1 us
    psum x1, waiting for transfers between devices, on_device(): energy = lax.psum(local_energy, 'tm') / (cycle * frames_all) + 1e-06  62.9 us
    another operation x65, local copies, waits for them, and re-layouts, cycle_passes(): jnp.stack([jnp.sum(error_part * window_of(padded, point, height, width),...  60.1 us
    reduce_sum x4, other arithmetic, cycle_passes(): jnp.sum(error_part * window_of(padded, point, height, width), axis=0)  15.2 us
    dot_general x1, matrix products, reorder(): jnp.einsum('jk,kyx->jyx', selector, weights, precision=lax.Precision.HIGH...  13.4 us
  transfers between devices with their start and end apart: 5, of which 4 were waited for; matrix products, arithmetic and copies ran while one was open for 28% of the time, Pallas kernels for 0%

commit v1 on v0

--- a/solution.py
+++ b/solution.py
@@ -79,7 +79,12 @@
     extended = with_halo(residual, (("rows", 1),), 6)
     padded = jnp.pad(extended, ((0, 0), (0, 0), (6, 6)))
     columns = selector
-    ordered_weight = reorder(columns, lax.all_gather(cycle_weight, "tm", axis=0, tiled=True))
+    ordered_weight = reorder(
+        columns,
+        jnp.concatenate(
+            lax.all_to_all(jnp.stack([cycle_weight] * lax.axis_size("tm")), "tm", 0, 0), axis=0
+        ),
+    )
     error, ordered_grad, local_energy = cycle_passes(
         padded, residual, ordered_weight, points, rows_dev, cols
     )

time: 434 us -> 536 us (1.24)
  waiting for transfers between devices: 289 us -> 360 us
  local copies, waits for them, and re-layouts: 79 us -> 103 us
  starting transfers between devices: 3.62 us -> 14.7 us
  matrix products: 21.6 us -> 16.1 us
    all_to_all x0 -> x1, waiting for transfers between devices: none -> 176 us  [on_device(): lax.all_to_all(jnp.stack([cycle_weight] * lax.axis_size('tm')), 'tm', 0, 0)]
    all_gather x1 -> x0, waiting for transfers between devices: 97.1 us -> none  [on_device(): lax.all_gather(cycle_weight, 'tm', axis=0, tiled=True)]
    all_to_all x0 -> x1, starting transfers between devices: none -> 11.6 us  [on_device(): lax.all_to_all(jnp.stack([cycle_weight] * lax.axis_size('tm')), 'tm', 0, 0)]
    reshape x0 -> x1, local copies, waits for them, and re-layouts: none -> 10 us  [on_device(): jnp.concatenate(lax.all_to_all(jnp.stack([cycle_weight] * lax.axis_size('...]
    all_to_all x0 -> x1, local copies, waits for them, and re-layouts: none -> 9.2 us  [on_device(): lax.all_to_all(jnp.stack([cycle_weight] * lax.axis_size('tm')), 'tm', 0, 0)]
    psum x1, waiting for transfers between devices: 62.9 us -> 54 us  [on_device(): energy = lax.psum(local_energy, 'tm') / (cycle * frames_all) + 1e-06]
    dot_general x1, matrix products: 13.4 us -> 7.95 us  [reorder(): jnp.einsum('jk,kyx->jyx', selector, weights, precision=lax.Precision.HIGH...]
  transfers between devices with their start and end apart: 5 -> 5, of which waited for: 4 -> 4; matrix products, arithmetic and copies ran while one was open for 28% -> 25% of each run, Pallas kernels for 0% -> 0%
where the time goes in v1:
time: 536 us; the launch traced here: 530 us
  waiting for transfers between devices  360 us (67%)
  local copies, waits for them, and re-layouts  103 us (19%)
  other arithmetic  21.4 us (4%)
  matrix products  16.1 us (3%)
  between operations  14.9 us (3%)
  starting transfers between devices  14.7 us (3%)
    all_to_all x1, waiting for transfers between devices, on_device(): lax.all_to_all(jnp.stack([cycle_weight] * lax.axis_size('tm')), 'tm', 0, 0)  176 us
    reduce_scatter x1, waiting for transfers between devices, on_device(): lax.psum_scatter(jnp.einsum('jk,jyx->kyx', columns, ordered_grad, precisi...  127 us
    another operation x65, local copies, waits for them, and re-layouts, cycle_passes(): jnp.stack([jnp.sum(error_part * window_of(padded, point, height, width),...  60.4 us
    psum x1, waiting for transfers between devices, on_device(): energy = lax.psum(local_energy, 'tm') / (cycle * frames_all) + 1e-06  54 us
    reduce_sum x4, other arithmetic, cycle_passes(): jnp.sum(error_part * window_of(padded, point, height, width), axis=0)  15.3 us
    all_to_all x1, starting transfers between devices, on_device(): lax.all_to_all(jnp.stack([cycle_weight] * lax.axis_size('tm')), 'tm', 0, 0)  11.6 us
  transfers between devices with their start and end apart: 5, of which 4 were waited for; matrix products, arithmetic and copies ran while one was open for 25% of the time, Pallas kernels for 0%

profile of v1, /device:TPU:4, one launch (start us, length us, event | category | flops | bytes accessed | tf_op | source)
XLA Modules:
  0.0 530.1 jit_solution(7993910399045011845)
XLA Ops:
  7.2 1.4 copy.11
  8.5 4.8 stack.214
  13.4 11.6 %all-to-all-start = ((f32[16,4,64,512]{3,1,2,0:T(4,128)}), f32[16,4,64,512]{3,1,2,0:T(4,128)}, u32[]{:S(2)}, u32[]{:S(2)}) async-start(f32[16,4,64,512]{3,1,2,0:T(4,128)} %stack.214), calls=%async_computation | async-start | bytes 16777216 | tf_op jit(solution)/shard_map/all_to_all | solution.py:85
  25.0 1.3 collective-permute-start
  26.3 1.3 collective-permute-start.1
  27.7 3.6 collective-permute-done.1
  31.6 2.9 slice_add_fusion
  35.0 175.8 %all-to-all-done = f32[16,4,64,512]{3,1,2,0:T(4,128)} async-done(((f32[16,4,64,512]{3,1,2,0:T(4,128)}), f32[16,4,64,512]{3,1,2,0:T(4,128)}, u32[]{:S(2)}, u32[]{:S(2)}) %all-to-all-start) | async-done | bytes 8388640 | tf_op jit(solution)/shard_map/all_to_all | solution.py:85
  210.9 9.2 %copy.12 = f32[16,4,64,512]{3,1,0,2:T(4,128)} copy(f32[16,4,64,512]{3,1,2,0:T(4,128)} %all-to-all-done) | data formatting | bytes 16777216 | tf_op jit(solution)/shard_map/all_to_all | solution.py:85
  220.1 10.0 %reshape.14 = f32[64,64,512]{2,0,1:T(8,128)} reshape(f32[16,4,64,512]{3,1,0,2:T(4,128)} %copy.12) | data formatting | bytes 16777216 | tf_op jit(solution)/shard_map/reshape | solution.py:84
  230.1 7.9 %fusion.2 = f32[64,64,512]{2,0,1:T(8,128)S(1)} fusion(f32[64,64,512]{2,0,1:T(8,128)} %reshape.14, s32[64]{0:T(128)S(1)} %copy-done.4, s32[64]{0:T(128)S(1)} %copy-done.3, s32[64]{0:T(128)S(1)} %get-tuple-element.146, s32[64]{0:T(128)S(1)} %get-tuple-element.145), kind=kOutput, calls=%fused_computation.204 | convolution fusion | flops 1610625024 | bytes 16778240 | tf_op jit(solution)/shard_map/jk,kyx->jyx/dot_general | solution.py:45
  238.1 2.3 fusion.14
  240.4 2.5 fusion.15
  242.9 2.5 fusion.16
  246.9 9.6 %multiply_reduce_fusion.2 = (f32[64,512]{1,0:T(8,128)S(1)}, f32[64,512]{1,0:T(8,128)S(1)}, f32[64,512]{1,0:T(8,128)S(1)}, f32[64,512]{1,0:T(8,128)S(1)}, f32[64,...) fusion(f32[4,76,524]{2,1,0:T(8,128)S(1)} %get-tuple-element.142, ...), kind=kLoop, calls=%fused_computation.12 | loop fusion | flops 21168128 | bytes 44351488 | tf_op jit(solution)/shard_map/reduce_sum | solution.py:60
  256.5 2.5 multiply_reduce_fusion.39
  259.0 2.4 multiply_reduce_fusion.21
  262.1 0.7 stack.230
  262.9 0.7 stack.231
  264.3 0.7 stack.233
  265.8 0.7 stack.235
  266.5 0.7 stack.236
  267.3 0.7 stack.237
  268.0 0.7 stack.238
  268.8 0.7 stack.239
  271.0 0.7 stack.242
  272.5 0.7 stack.244
  273.2 0.7 stack.245
  273.9 0.7 stack.246
  275.4 0.7 stack.248
  276.2 0.7 stack.249
  276.9 0.7 stack.250
  277.6 0.7 stack.251
  278.4 0.7 stack.252
  281.3 0.7 stack.256
  283.5 0.9 multiply_reduce_fusion.1
  288.5 0.8 stack.271
  289.3 0.7 stack.272
  290.8 0.9 stack.275
  291.7 0.7 stack.276
  292.4 0.7 stack.277
  293.2 29.8 %stack.279 = f32[64,64,512]{2,0,1:T(8,128)} concatenate(f32[1,64,512]{2,0,1:T(1,128)S(1)} %stack.215, f32[1,64,512]{2,0,1:T(1,128)S(1)} %stack.216, f32[1,64,512]{2,0,1:T(1,128)S(1)} %stack.217, f32[1,64,512]{2,0,1:T(1,128)S(1)} %stack.218, f32[1,64,512]{2,0,1:T(1,128)S(1)} %stack.219, f32[1,64,512]{2,0,1:T(1,128)S(1)} %stack.220, f32[1,64,512]{2,0,1:T(1,128)S(1)} %stack.221, ...), dimensions={0} | concatenate | bytes 16777216 | tf_op jit(solution)/shard_map/stack | solution.py:59
  322.9 8.2 %fusion.4 = f32[64,64,512]{2,0,1:T(8,128)S(1)} fusion(f32[64,64,512]{2,0,1:T(8,128)} %stack.279, s32[64]{0:T(128)S(1)} %copy-done.4, s32[64]{0:T(128)S(1)} %copy-done.3, s32[64]{0:T(128)S(1)} %get-tuple-element.146, s32[64]{0:T(128)S(1)} %get-tuple-element.145), kind=kOutput, calls=%fused_computation.206 | convolution fusion | flops 1610625024 | bytes 16778240 | tf_op jit(solution)/shard_map/jk,jyx->kyx/dot_general | solution.py:93
  331.1 8.1 %copy.14 = f32[64,64,512]{2,1,0:T(8,128)} copy(f32[64,64,512]{2,0,1:T(8,128)S(1)} %fusion.4) | data formatting | bytes 16777216 | tf_op jit(solution)/shard_map/jk,jyx->kyx/dot_general | solution.py:93
  339.2 54.0 %all-reduce.3.cloned.1.call-done = f32[64,512]{1,0:T(8,128)} async-done(((f32[64,512]{1,0:T(8,128)}), f32[64,512]{1,0:T(8,128)}) %all-reduce.3.cloned.1.call-update) | async-done | bytes 131088 | tf_op jit(solution)/shard_map/psum | solution.py:98
  393.2 0.9 add_multiply_fusion
  394.1 127.0 %reduce-scatter.2.cloned.1.call-done = f32[4,64,512]{2,1,0:T(8,128)} async-done(((f32[64,64,512]{2,1,0:T(8,128)}), f32[4,64,512]{2,1,0:T(8,128)}) %reduce-scatter.2.cloned.1.call-update) | async-done | bytes 524304 | tf_op jit(solution)/shard_map/reduce_scatter | solution.py:92
  521.1 1.9 divide_add_fusion
  (96 shorter events, 15.6 us)
Async XLA Ops:
  13.4 11.6 %copy-start = (f32[4,64,512]{2,1,0:T(8,128)S(1)}, f32[4,64,512]{2,1,0:T(8,128)}, u32[]{:S(2)}) copy-start(f32[4,64,512]{2,1,0:T(8,128)} %param.5) | copy-start | bytes 1572868
  13.4 14.3 %copy-start.5 = (s32[64,2]{0,1:T(2,128)S(1)}, s32[64,2]{0,1:T(2,128)}, u32[]{:S(2)}) copy-start(s32[64,2]{0,1:T(2,128)} %param.7) | copy-start | bytes 1540
  13.4 197.5 %all-to-all-start = ((f32[16,4,64,512]{3,1,2,0:T(4,128)}), f32[16,4,64,512]{3,1,2,0:T(4,128)}, u32[]{:S(2)}, u32[]{:S(2)}) async-start(f32[16,4,64,512]{3,1,2,0:T(4,128)} %stack.214), calls=%async_computation | async-start | bytes 16777216 | tf_op jit(solution)/shard_map/all_to_all | solution.py:85
  25.0 368.2 %all-reduce.3.cloned.1.call-start = ((), (), s32[]{:S(2)}) async-start(), calls=%async_computation.3 | async-start | bytes 262144 | tf_op jit(solution)/shard_map/psum | solution.py:98
  25.0 2.7 collective-permute-start
  26.3 5.0 collective-permute-start.1
  34.5 486.6 %reduce-scatter.2.cloned.1.call-start = ((), (), s32[]{:S(2)}) async-start(), calls=%async_computation.2 | async-start | bytes 8912896 | tf_op jit(solution)/shard_map/reduce_scatter | solution.py:92
  220.1 10.0 %copy-start.3 = (s32[64]{0:T(128)S(1)}, s32[64]{0:T(128)}, u32[]{:S(2)}) copy-start(s32[64]{0:T(128)} %constant.15.clone) | copy-start | bytes 772
  220.1 10.0 %copy-start.4 = (s32[64]{0:T(128)S(1)}, s32[64]{0:T(128)}, u32[]{:S(2)}) copy-start(s32[64]{0:T(128)} %constant.16.clone) | copy-start | bytes 772
  256.5 27.0 %copy-start.1 = (f32[4,64,512]{2,1,0:T(8,128)}, f32[4,64,512]{2,1,0:T(8,128)S(1)}, u32[]{:S(2)}) copy-start(f32[4,64,512]{2,1,0:T(8,128)S(1)} %get-tuple-element.76) | copy-start | bytes 1572868
  339.2 181.9 %copy-start.2 = (f32[4,64,512]{2,1,0:T(8,128)S(1)}, f32[4,64,512]{2,1,0:T(8,128)}, u32[]{:S(2)}) copy-start(f32[4,64,512]{2,1,0:T(8,128)} %param.6) | copy-start | bytes 1572868
Sparse Core Ops, SparseCore 0:
  34.6 358.4 all-reduce.2
  396.9 124.1 reduce-scatter.1
